TPU v7x, 128 devices: a whole 4x4x4 slice. The times are simulated.
128 devices in a mesh: seq: 8 (over z, core), exp: 16 (over y, x).
Axes of the slice: x: 4, y: 4, z: 4, core: 2. Of those that a mesh axis runs over, the one named last changes fastest.
Arguments:
- attn_query: bfloat16 [2048, 6144], P('seq', 'exp'), may hold values from -6 to 6
- attn_key: bfloat16 [2048, 6144], P('seq', 'exp'), may hold values from -6 to 6
- attn_value: bfloat16 [2048, 6144], P('seq', 'exp'), may hold values from -40 to 40
- log_decay: float32 [48, 2048], P('exp', 'seq'), may hold values from -1.5 to 0
- residual: bfloat16 [2048, 6144], P('seq', 'exp'), may hold values from -6 to 6
- norm_gain: bfloat16 [6144], P('exp'), may hold values from 0.099609375 to 1.8984375
- expert_ids: int32 [2048, 2], P('seq'), may hold values from 0 to 15, as said below
- router_weight: bfloat16 [6144, 16], P(None, 'seq'), may hold values from -0.078125 to 0.078125
- gate_weight: bfloat16 [16, 6144, 4608], P('seq', None, 'exp'), may hold values from -0.078125 to 0.078125
- up_weight: bfloat16 [16, 6144, 4608], P('seq', None, 'exp'), may hold values from -0.078125 to 0.078125
- down_weight: bfloat16 [16, 4608, 6144], P('seq', 'exp'), may hold values from -0.125 to 0.125
Outputs:
- layer_out: bfloat16 [2048, 6144], P('seq', 'exp')
Inputs may be any that keep to these rules, and one draw needn't show every extreme that they name: `expert_ids`: each row names two different experts. In every section of 256 consecutive rows no expert is named more than 64 times, and in every section some experts are named exactly 64 times.
All inputs are finite; a program needn't handle non-finite values.
Results may differ from a plain program's by a relative error of at most 0.017.
Values may be sent and summed in bfloat16 or wider, within the bound.
A program may use at most 192 MiB of HBM per device.

v0:
```python
import jax
import jax.numpy as jnp
from jax import lax
from jax.sharding import PartitionSpec as P


def shifted(array, axis, by):
    count = lax.axis_size(axis)
    pairs = [(i, i + by) for i in range(count) if 0 <= i + by < count]
    return lax.ppermute(array, axis, pairs)


def on_device(
    attn_query,
    attn_key,
    attn_value,
    log_decay,
    residual,
    norm_gain,
    expert_ids,
    router_weight,
    gate_weight,
    up_weight,
    down_weight,
):
    heads_here = log_decay.shape[0]
    length = log_decay.shape[1]
    head_size = attn_query.shape[1] // heads_here
    query_rows = attn_query.reshape(length, heads_here, head_size)
    key_rows = attn_key.reshape(length, heads_here, head_size)
    value_rows = attn_value.reshape(length, heads_here, head_size)
    cumulative = jnp.cumsum(log_decay, axis=1)
    causal = lax.broadcasted_iota(jnp.int32, (length, length), 0) >= lax.broadcasted_iota(
        jnp.int32, (length, length), 1
    )
    decay_gap = jnp.where(causal[None], cumulative[:, :, None] - cumulative[:, None, :], 0.0)
    decay_mask = jnp.where(causal[None], jnp.exp(decay_gap), 0.0)
    scores = jnp.einsum("thd,shd->hts", query_rows, key_rows, preferred_element_type=jnp.float32)
    weights = (scores * decay_mask).astype(jnp.bfloat16)
    intra_part = jnp.einsum("hts,shd->thd", weights, value_rows, preferred_element_type=jnp.float32)
    key_fade = jnp.exp(cumulative[:, -1:] - cumulative)
    scaled = (key_fade.T[:, :, None] * key_rows.astype(jnp.float32)).astype(jnp.bfloat16)
    local_state = jnp.einsum("shd,she->hde", scaled, value_rows, preferred_element_type=jnp.float32)
    section_fade = jnp.exp(cumulative[:, -1])
    incoming = jnp.zeros_like(local_state)
    for repeat_index in range(lax.axis_size("seq") - 1):
        incoming = shifted(section_fade[:, None, None] * incoming + local_state, "seq", 1)
    inter_part = jnp.einsum(
        "thd,hde->the", query_rows.astype(jnp.float32), incoming, precision=lax.Precision.HIGHEST
    )
    attn_out = intra_part + jnp.exp(cumulative).T[:, :, None] * inter_part
    mean_square = jnp.mean(attn_out * attn_out, axis=2, keepdims=True)
    normed = (attn_out / jnp.sqrt(mean_square + 1e-06)).reshape(length, heads_here * head_size)
    stream = (residual.astype(jnp.float32) + norm_gain.astype(jnp.float32) * normed).astype(
        jnp.bfloat16
    )
    experts_here = router_weight.shape[1]
    groups = lax.axis_size("seq")
    expert_count = experts_here * groups
    capacity = 4 * length // expert_count
    features = stream.shape[1]
    choices_per_token = expert_ids.shape[1]
    flat_ids = expert_ids.reshape(-1)
    expert_iota = lax.broadcasted_iota(jnp.int32, (1, expert_count), 1)
    onehot = (flat_ids[:, None] == expert_iota).astype(jnp.int32)
    running = jnp.cumsum(onehot, axis=0)
    slot_index = jnp.sum(running * onehot, axis=1) - 1
    target = flat_ids * capacity + slot_index
    place_iota = lax.broadcasted_iota(jnp.int32, (expert_count * capacity, 1), 0)
    route_matrix = (
        (place_iota == target[None, :])
        .astype(jnp.bfloat16)
        .reshape(expert_count * capacity, length, choices_per_token)
        .sum(axis=2)
    )
    outgoing = jnp.dot(route_matrix, stream, preferred_element_type=jnp.float32).astype(
        jnp.bfloat16
    )
    outgoing = outgoing.reshape(groups, experts_here, capacity, features)
    portion = lax.all_gather(
        lax.all_to_all(outgoing, "seq", split_axis=0, concat_axis=0, tiled=True),
        "exp",
        axis=3,
        tiled=True,
    )
    gate_acc = jnp.einsum(
        "sjcd,jdf->sjcf", portion, gate_weight, preferred_element_type=jnp.float32
    )
    upward = jnp.einsum("sjcd,jdf->sjcf", portion, up_weight, preferred_element_type=jnp.float32)
    logits = jnp.einsum("sjcd,dj->sjc", portion, router_weight, preferred_element_type=jnp.float32)
    hidden_act = (jax.nn.silu(gate_acc) * upward).astype(jnp.bfloat16)
    expert_out = lax.psum_scatter(
        jnp.einsum(
            "sjcf,jfd->dsjc", hidden_act, down_weight, preferred_element_type=jnp.float32
        ).astype(jnp.bfloat16),
        "exp",
        scatter_dimension=0,
        tiled=True,
    ).astype(jnp.float32)
    routed = (jax.nn.sigmoid(logits)[None] * expert_out).astype(jnp.bfloat16)
    returned = lax.all_to_all(routed, "seq", split_axis=1, concat_axis=1, tiled=True)
    returned = returned.reshape(features, expert_count * capacity)
    combined = lax.dot_general(
        route_matrix, returned, (((0,), (1,)), ((), ())), preferred_element_type=jnp.float32
    )
    return (stream.astype(jnp.float32) + combined).astype(jnp.bfloat16)


def solution(mesh):
    in_specs = (
        P("seq", "exp"),
        P("seq", "exp"),
        P("seq", "exp"),
        P("exp", "seq"),
        P("seq", "exp"),
        P("exp"),
        P("seq", None),
        P(None, "seq"),
        P("seq", None, "exp"),
        P("seq", None, "exp"),
        P("seq", "exp", None),
    )
    out_specs = P("seq", "exp")
    return jax.shard_map(
        on_device, mesh=mesh, in_specs=in_specs, out_specs=out_specs, check_vma=False
    )
```

profile of v0, /device:TPU:1, one launch (start us, length us, event | category | flops | bytes accessed | tf_op | source)
XLA Modules:
  0.0 400.8 jit_solution(6427846024970069958)
XLA Ops:
  6.5 0.7 reshape.116
  7.3 0.9 reduce-window.14
  8.2 0.1 slice.21
  8.3 0.1 copy.83
  8.4 0.1 copy.84
  8.5 0.1 add_bitcast_fusion.1
  8.6 0.1 slice.22
  8.7 0.1 copy.109
  8.8 1.1 copy.80
  9.9 1.1 copy.85
  11.0 0.2 broadcast_add_fusion
  11.2 4.9 %collective-permute-start = (f32[3,128,128]{2,1,0:T(8,128)S(1)}, f32[3,128,128]{2,1,0:T(8,128)S(1)}, u32[]{:S(2)}, u32[]{:S(2)}) collective-permute-start(f32[3,128,128]{2,1,0:T(8,128)S(1)} %get-tuple-element.9), channel_id=1, source_target_pairs={{0,16},{16,32},{32,48},{48,64},{64,80},{80,96},{96,112},{1,17},{17... | collective-permute-start | bytes 589832 | tf_op jit(solution)/shard_map/ppermute | solution.py:10
  16.1 0.8 copy.91
  17.0 0.1 eq.44
  17.1 0.1 eq.40
  17.3 0.7 convert_element_type.55
  17.9 0.8 collective-permute-done
  18.7 0.1 multiply_add_fusion.5
  18.8 4.4 %collective-permute-start.1 = (f32[3,128,128]{2,1,0:T(8,128)S(1)}, f32[3,128,128]{2,1,0:T(8,128)S(1)}, u32[]{:S(2)}, u32[]{:S(2)}) collective-permute-start(f32[3,128,128]{2,1,0:T(8,128)S(1)} %multiply_add_fusion.5), channel_id=1, source_target_pairs={{0,16},{16,32},{32,48},{48,64},{64,80},{80,96},{96,112},{1,17},{17... | collective-permute-start | bytes 589832 | tf_op jit(solution)/shard_map/ppermute | solution.py:10
  23.2 1.2 reduce-window.16
  24.4 1.4 collective-permute-done.1
  25.8 0.1 multiply_add_fusion.4
  25.9 4.4 %collective-permute-start.2 = (f32[3,128,128]{2,1,0:T(8,128)S(1)}, f32[3,128,128]{2,1,0:T(8,128)S(1)}, u32[]{:S(2)}, u32[]{:S(2)}) collective-permute-start(f32[3,128,128]{2,1,0:T(8,128)S(1)} %multiply_add_fusion.4), channel_id=1, source_target_pairs={{0,16},{16,32},{32,48},{48,64},{64,80},{80,96},{96,112},{1,17},{17... | collective-permute-start | bytes 589832 | tf_op jit(solution)/shard_map/ppermute | solution.py:10
  30.3 0.2 slice_reduce_fusion
  30.6 0.1 fusion.32
  30.7 2.2 collective-permute-done.2
  32.9 0.1 multiply_add_fusion.3
  33.0 4.4 %collective-permute-start.3 = (f32[3,128,128]{2,1,0:T(8,128)S(1)}, f32[3,128,128]{2,1,0:T(8,128)S(1)}, u32[]{:S(2)}, u32[]{:S(2)}) collective-permute-start(f32[3,128,128]{2,1,0:T(8,128)S(1)} %multiply_add_fusion.3), channel_id=1, source_target_pairs={{0,16},{16,32},{32,48},{48,64},{64,80},{80,96},{96,112},{1,17},{17... | collective-permute-start | bytes 589832 | tf_op jit(solution)/shard_map/ppermute | solution.py:10
  37.4 0.1 sub.33
  37.5 0.1 copy.94
  37.6 1.1 copy.79
  38.7 1.3 collective-permute-done.3
  40.0 0.1 multiply_add_fusion.2
  40.1 4.4 %collective-permute-start.4 = (f32[3,128,128]{2,1,0:T(8,128)S(1)}, f32[3,128,128]{2,1,0:T(8,128)S(1)}, u32[]{:S(2)}, u32[]{:S(2)}) collective-permute-start(f32[3,128,128]{2,1,0:T(8,128)S(1)} %multiply_add_fusion.2), channel_id=1, source_target_pairs={{0,16},{16,32},{32,48},{48,64},{64,80},{80,96},{96,112},{1,17},{17... | collective-permute-start | bytes 589832 | tf_op jit(solution)/shard_map/ppermute | solution.py:10
  44.5 0.7 multiply_add_fusion.6
  45.2 1.9 collective-permute-done.4
  47.1 0.1 multiply_add_fusion.1
  47.1 4.4 %collective-permute-start.5 = (f32[3,128,128]{2,1,0:T(8,128)S(1)}, f32[3,128,128]{2,1,0:T(8,128)S(1)}, u32[]{:S(2)}, u32[]{:S(2)}) collective-permute-start(f32[3,128,128]{2,1,0:T(8,128)S(1)} %multiply_add_fusion.1), channel_id=1, source_target_pairs={{0,16},{16,32},{32,48},{48,64},{64,80},{80,96},{96,112},{1,17},{17... | collective-permute-start | bytes 589832 | tf_op jit(solution)/shard_map/ppermute | solution.py:10
  51.6 0.5 fusion.18
  52.0 2.1 collective-permute-done.5
  54.1 0.1 multiply_add_fusion
  54.2 4.4 %collective-permute-start.6 = (f32[3,128,128]{2,1,0:T(8,128)S(1)}, f32[3,128,128]{2,1,0:T(8,128)S(1)}, u32[]{:S(2)}, u32[]{:S(2)}) collective-permute-start(f32[3,128,128]{2,1,0:T(8,128)S(1)} %multiply_add_fusion), channel_id=1, source_target_pairs={{0,16},{16,32},{32,48},{48,64},{64,80},{80,96},{96,112},{1,17},{17... | collective-permute-start | bytes 589832 | tf_op jit(solution)/shard_map/ppermute | solution.py:10
  58.6 0.5 fusion.14
  59.1 2.1 collective-permute-done.6
  61.2 0.4 multiply_reduce_fusion
  61.7 0.2 copy.90
  61.9 0.4 convolution_convert_fusion
  62.4 18.3 %all_to_all.10 = bf16[8,2,64,384]{3,2,1,0:T(8,128)(2,1)S(1)} all-to-all(bf16[8,2,64,384]{3,2,1,0:T(8,128)(2,1)S(1)} %bitcast.110), channel_id=1, replica_groups=mesh['seq'=8,'exp'=16] {'seq'}, dimensions={0} | all-to-all | bytes 1572864 | tf_op jit(solution)/shard_map/all_to_all | solution.py:81
  80.6 1.0 copy.95
  81.6 0.2 reduce-scatter.4.cloned.1.call-start
  81.9 98.5 %all-gather.2.cloned.1.call-done = bf16[8,2,64,6144]{3,2,0,1:T(8,128)(2,1)} async-done(((bf16[8,2,64,384]{3,2,0,1:T(8,128)(2,1)}), bf16[8,2,64,6144]{3,2,0,1:T(8,128)(2,1)}) %all-gather.2.cloned.1.call-update) | async-done | bytes 12582928 | tf_op jit(solution)/shard_map/all_gather | solution.py:80
  180.3 11.8 %fusion.3 = f32[2,8,64,288]{3,2,1,0:T(8,128)S(1)} fusion(bf16[8,2,64,6144]{3,2,0,1:T(8,128)(2,1)} %all-gather.2.cloned.1.call-done, bf16[2,6144,288]{1,2,0:T(8,128)(2,1)} %param.19), kind=kOutput, calls=%fused_computation.4 | convolution fusion | flops 3623878656 | bytes 20840448 | tf_op jit(solution)/shard_map/sjcd,jdf->sjcf/dot_general | solution.py:86
  192.1 8.9 %fusion.6 = bf16[8,2,64,288]{3,2,0,1:T(8,128)(2,1)S(1)} fusion(f32[2,8,64,288]{3,2,1,0:T(8,128)S(1)} %fusion.3, bf16[8,2,64,6144]{3,2,0,1:T(8,128)(2,1)S(1)} %copy-done.1, bf16[2,6144,288]{1,2,0:T(8,128)(2,1)} %param.20), kind=kOutput, calls=%fused_computation.9 | convolution fusion | flops 3625648128 | bytes 21430272 | tf_op jit(solution)/shard_map/sjcd,jdf->sjcf/dot_general | solution.py:89
  201.1 12.6 %convert_bitcast_fusion = bf16[6144,8,2,64]{0,3,1,2:T(8,128)(2,1)} fusion(bf16[8,2,64,288]{3,2,0,1:T(8,128)(2,1)S(1)} %fusion.6, bf16[2,288,6144]{2,1,0:T(8,128)(2,1)} %param.21), kind=kOutput, calls=%fused_computation | convolution fusion | flops 3630170112 | bytes 20250624 | tf_op jit(solution)/shard_map/sjcf,jfd->dsjc/dot_general | solution.py:93
  213.7 29.7 %copy.107 = bf16[6144,8,2,64]{3,1,2,0:T(8,128)(2,1)} copy(bf16[6144,8,2,64]{0,3,1,2:T(8,128)(2,1)} %convert_bitcast_fusion) | data formatting | bytes 25165824
  243.4 33.4 %reshape.128 = bf16[6144,1024]{1,0:T(8,128)(2,1)} reshape(bf16[6144,2,8,64]{3,2,1,0:T(8,128)(2,1)} %bitcast.108) | data formatting | bytes 25165824
  276.8 7.9 %fusion.29 = f32[2,1,8,64]{3,1,2,0:T(1,128)S(1)} fusion(bf16[8,2,64,6144]{3,2,0,1:T(8,128)(2,1)} %all-gather.2.cloned.1.call-done, bf16[6144,2,1,1]{0,1,2,3:T(2,128)(2,1)S(1)} %bitcast.107), kind=kOutput, calls=%fused_computation.49 | convolution fusion | flops 12582912 | bytes 12611584 | tf_op jit(solution)/shard_map/sjcd,dj->sjc/dot_general | solution.py:90
  284.7 86.8 %reduce-scatter.4.cloned.1.call-done = bf16[384,1024]{1,0:T(8,128)(2,1)} async-done(((bf16[6144,1024]{1,0:T(8,128)(2,1)}), bf16[384,1024]{1,0:T(8,128)(2,1)}) %reduce-scatter.4.cloned.1.call-update) | async-done | bytes 786448
  371.5 2.5 reshape.129
  374.0 1.2 copy.108
  375.2 0.2 multiply_convert_fusion
  375.4 0.1 copy.96
  375.5 17.3 %all_to_all.11 = bf16[384,8,2,64]{0,3,2,1:T(8,128)(2,1)S(1)} all-to-all(bf16[384,8,2,64]{0,3,2,1:T(8,128)(2,1)S(1)} %copy.96), channel_id=1, replica_groups=mesh['seq'=8,'exp'=16] {'seq'}, dimensions={1} | all-to-all | bytes 1572864 | tf_op jit(solution)/shard_map/all_to_all | solution.py:101
  392.8 1.1 fusion.17
  (23 shorter events, 0.4 us)
Async XLA Ops:
  6.5 270.3 %copy-start = (bf16[6144,2]{0,1:T(2,128)(2,1)S(1)}, bf16[6144,2]{0,1:T(2,128)(2,1)}, u32[]{:S(2)}) copy-start(bf16[6144,2]{0,1:T(2,128)(2,1)} %param.18) | copy-start | bytes 73732
  6.5 55.3 %copy-start.2 = (bf16[256,384]{1,0:T(8,128)(2,1)S(1)}, bf16[256,384]{1,0:T(8,128)(2,1)}, u32[]{:S(2)}) copy-start(bf16[256,384]{1,0:T(8,128)(2,1)} %param.15) | copy-start | bytes 589828
  6.5 173.8 %all-gather.2.cloned.1.call-start = ((), (), s32[]{:S(2)}) async-start(), calls=%async_computation.3 | async-start | bytes 13369344 | tf_op jit(solution)/shard_map/all_gather | solution.py:80
  11.2 7.5 %collective-permute-start = (f32[3,128,128]{2,1,0:T(8,128)S(1)}, f32[3,128,128]{2,1,0:T(8,128)S(1)}, u32[]{:S(2)}, u32[]{:S(2)}) collective-permute-start(f32[3,128,128]{2,1,0:T(8,128)S(1)} %get-tuple-element.9), channel_id=1, source_target_pairs={{0,16},{16,32},{32,48},{48,64},{64,80},{80,96},{96,112},{1,17},{17... | collective-permute-start | bytes 589832 | tf_op jit(solution)/shard_map/ppermute | solution.py:10
  18.8 7.0 %collective-permute-start.1 = (f32[3,128,128]{2,1,0:T(8,128)S(1)}, f32[3,128,128]{2,1,0:T(8,128)S(1)}, u32[]{:S(2)}, u32[]{:S(2)}) collective-permute-start(f32[3,128,128]{2,1,0:T(8,128)S(1)} %multiply_add_fusion.5), channel_id=1, source_target_pairs={{0,16},{16,32},{32,48},{48,64},{64,80},{80,96},{96,112},{1,17},{17... | collective-permute-start | bytes 589832 | tf_op jit(solution)/shard_map/ppermute | solution.py:10
  25.9 7.0 %collective-permute-start.2 = (f32[3,128,128]{2,1,0:T(8,128)S(1)}, f32[3,128,128]{2,1,0:T(8,128)S(1)}, u32[]{:S(2)}, u32[]{:S(2)}) collective-permute-start(f32[3,128,128]{2,1,0:T(8,128)S(1)} %multiply_add_fusion.4), channel_id=1, source_target_pairs={{0,16},{16,32},{32,48},{48,64},{64,80},{80,96},{96,112},{1,17},{17... | collective-permute-start | bytes 589832 | tf_op jit(solution)/shard_map/ppermute | solution.py:10
  33.0 7.0 %collective-permute-start.3 = (f32[3,128,128]{2,1,0:T(8,128)S(1)}, f32[3,128,128]{2,1,0:T(8,128)S(1)}, u32[]{:S(2)}, u32[]{:S(2)}) collective-permute-start(f32[3,128,128]{2,1,0:T(8,128)S(1)} %multiply_add_fusion.3), channel_id=1, source_target_pairs={{0,16},{16,32},{32,48},{48,64},{64,80},{80,96},{96,112},{1,17},{17... | collective-permute-start | bytes 589832 | tf_op jit(solution)/shard_map/ppermute | solution.py:10
  40.1 7.0 %collective-permute-start.4 = (f32[3,128,128]{2,1,0:T(8,128)S(1)}, f32[3,128,128]{2,1,0:T(8,128)S(1)}, u32[]{:S(2)}, u32[]{:S(2)}) collective-permute-start(f32[3,128,128]{2,1,0:T(8,128)S(1)} %multiply_add_fusion.2), channel_id=1, source_target_pairs={{0,16},{16,32},{32,48},{48,64},{64,80},{80,96},{96,112},{1,17},{17... | collective-permute-start | bytes 589832 | tf_op jit(solution)/shard_map/ppermute | solution.py:10
  47.1 7.0 %collective-permute-start.5 = (f32[3,128,128]{2,1,0:T(8,128)S(1)}, f32[3,128,128]{2,1,0:T(8,128)S(1)}, u32[]{:S(2)}, u32[]{:S(2)}) collective-permute-start(f32[3,128,128]{2,1,0:T(8,128)S(1)} %multiply_add_fusion.1), channel_id=1, source_target_pairs={{0,16},{16,32},{32,48},{48,64},{64,80},{80,96},{96,112},{1,17},{17... | collective-permute-start | bytes 589832 | tf_op jit(solution)/shard_map/ppermute | solution.py:10
  54.2 7.0 %collective-permute-start.6 = (f32[3,128,128]{2,1,0:T(8,128)S(1)}, f32[3,128,128]{2,1,0:T(8,128)S(1)}, u32[]{:S(2)}, u32[]{:S(2)}) collective-permute-start(f32[3,128,128]{2,1,0:T(8,128)S(1)} %multiply_add_fusion), channel_id=1, source_target_pairs={{0,16},{16,32},{32,48},{48,64},{64,80},{80,96},{96,112},{1,17},{17... | collective-permute-start | bytes 589832 | tf_op jit(solution)/shard_map/ppermute | solution.py:10
  81.6 289.9 %reduce-scatter.4.cloned.1.call-start = ((), (), s32[]{:S(2)}) async-start(), calls=%async_computation.4 | async-start | bytes 13369344
  180.3 11.8 %copy-start.1 = (bf16[8,2,64,6144]{3,2,0,1:T(8,128)(2,1)S(1)}, bf16[8,2,64,6144]{3,2,0,1:T(8,128)(2,1)}, u32[]{:S(2)}) copy-start(bf16[8,2,64,6144]{3,2,0,1:T(8,128)(2,1)} %all-gather.2.cloned.1.call-done) | copy-start | bytes 37748740
Sparse Core Ops, SparseCore 0:
  81.7 98.5 all-gather.1
  276.9 94.5 reduce-scatter.3
where the time goes:
time: 403 us; the launch traced here: 401 us
  waiting for transfers between devices  197 us (49%)
  local copies, waits for them, and re-layouts  73.9 us (18%)
  matrix products  43.9 us (11%)
  blocking collectives  35.6 us (9%)
  starting transfers between devices  31.5 us (8%)
  between operations  13.7 us (3%)
  other arithmetic  5.1 us (1%)
    all_gather x1, waiting for transfers between devices, on_device(): lax.all_gather(lax.all_to_all(outgoing, 'seq', split_axis=0, concat_axis=...  98.5 us
    unnamed x3, waiting for transfers between devices  86.8 us
    unnamed x16, local copies, waits for them, and re-layouts  70.9 us
    ppermute x7, starting transfers between devices, shifted(): return lax.ppermute(array, axis, pairs)  31.3 us
    all_to_all x1, blocking collectives, on_device(): lax.all_to_all(outgoing, 'seq', split_axis=0, concat_axis=0, tiled=True)  18.3 us
    all_to_all x1, blocking collectives, on_device(): lax.all_to_all(routed, 'seq', split_axis=1, concat_axis=1, tiled=True)  17.3 us
    dot_general x1, matrix products, on_device(): jnp.einsum('sjcf,jfd->dsjc', hidden_act, down_weight, preferred_element_t...  12.6 us
    dot_general x1, matrix products, on_device(): jnp.einsum('sjcd,jdf->sjcf', portion, gate_weight, preferred_element_type...  11.8 us
  transfers between devices with their start and end apart: 9, of which 9 were waited for; matrix products, arithmetic and copies ran while one was open for 4% of the time, Pallas kernels for 0%

commit v1 on v0

--- a/solution.py
+++ b/solution.py
@@ -77,11 +77,18 @@
         jnp.bfloat16
     )
     outgoing = outgoing.reshape(groups, experts_here, capacity, features)
-    portion = lax.all_gather(
-        lax.all_to_all(outgoing, "seq", split_axis=0, concat_axis=0, tiled=True),
-        "exp",
-        axis=3,
-        tiled=True,
+    portion = jnp.concatenate(
+        lax.all_to_all(
+            jnp.stack(
+                lax.axis_size("exp")
+                * [lax.all_to_all(outgoing, "seq", split_axis=0, concat_axis=0, tiled=True)],
+                0,
+            ),
+            axis_name="exp",
+            concat_axis=0,
+            split_axis=0,
+        ),
+        3,
     )
     gate_acc = jnp.einsum(
         "sjcd,jdf->sjcf", portion, gate_weight, preferred_element_type=jnp.float32

time: 403 us -> 456 us (1.13)
  blocking collectives: 35.6 us -> 182 us
  waiting for transfers between devices: 197 us -> 95.4 us
  local copies, waits for them, and re-layouts: 73.9 us -> 83 us
    all_to_all x0 -> x1, blocking collectives: none -> 146 us  [on_device(): lax.all_to_all(jnp.stack(lax.axis_size('exp') * [lax.all_to_all(outgoing,...]
    all_gather x1 -> x0, waiting for transfers between devices: 98.5 us -> none  [on_device(): lax.all_gather(lax.all_to_all(outgoing, 'seq', split_axis=0, concat_axis=...]
    another operation x4 -> x5, local copies, waits for them, and re-layouts: 0.32 us -> 7.02 us  [the longest x1 6.7 us: on_device(): jnp.stack(lax.axis_size('exp') * [lax.all_to_all(outgoing, 'seq', split_a...]
    unnamed x3 -> x2, waiting for transfers between devices: 86.8 us -> 83.6 us
  transfers between devices with their start and end apart: 9 -> 8, of which waited for: 9 -> 8; matrix products, arithmetic and copies ran while one was open for 4% -> 3% of each run, Pallas kernels for 0% -> 0%
where the time goes in v1:
time: 456 us; the launch traced here: 454 us
  blocking collectives  182 us (40%)
  waiting for transfers between devices  95.4 us (21%)
  local copies, waits for them, and re-layouts  83 us (18%)
  matrix products  43.6 us (10%)
  starting transfers between devices  31.3 us (7%)
  between operations  13.7 us (3%)
  other arithmetic  5.1 us (1%)
    all_to_all x1, blocking collectives, on_device(): lax.all_to_all(jnp.stack(lax.axis_size('exp') * [lax.all_to_all(outgoing,...  146 us
    unnamed x2, waiting for transfers between devices  83.6 us
    unnamed x16, local copies, waits for them, and re-layouts  70.9 us
    ppermute x7, starting transfers between devices, shifted(): return lax.ppermute(array, axis, pairs)  31.3 us
    all_to_all x1, blocking collectives, on_device(): lax.all_to_all(outgoing, 'seq', split_axis=0, concat_axis=0, tiled=True)  18.3 us
    all_to_all x1, blocking collectives, on_device(): lax.all_to_all(routed, 'seq', split_axis=1, concat_axis=1, tiled=True)  17.3 us
    dot_general x1, matrix products, on_device(): jnp.einsum('sjcf,jfd->dsjc', hidden_act, down_weight, preferred_element_t...  12.6 us
    ppermute x7, waiting for transfers between devices, shifted(): return lax.ppermute(array, axis, pairs)  11.8 us
  transfers between devices with their start and end apart: 8, of which 8 were waited for; matrix products, arithmetic and copies ran while one was open for 3% of the time, Pallas kernels for 0%

profile of v1, /device:TPU:1, one launch (start us, length us, event | category | flops | bytes accessed | tf_op | source)
XLA Modules:
  0.0 453.9 jit_solution(14732031231389235297)
XLA Ops:
  6.5 0.7 reshape.124
  7.3 0.9 reduce-window.14
  8.2 0.1 slice.21
  8.3 0.1 copy.85
  8.4 0.1 copy.86
  8.5 0.1 add_bitcast_fusion.1
  8.6 0.1 slice.22
  8.7 0.1 copy.112
  8.8 1.1 copy.82
  9.9 1.1 copy.87
  11.0 0.2 broadcast_add_fusion
  11.2 4.9 %collective-permute-start = (f32[3,128,128]{2,1,0:T(8,128)S(1)}, f32[3,128,128]{2,1,0:T(8,128)S(1)}, u32[]{:S(2)}, u32[]{:S(2)}) collective-permute-start(f32[3,128,128]{2,1,0:T(8,128)S(1)} %get-tuple-element.9), channel_id=1, source_target_pairs={{0,16},{16,32},{32,48},{48,64},{64,80},{80,96},{96,112},{1,17},{17... | collective-permute-start | bytes 589832 | tf_op jit(solution)/shard_map/ppermute | solution.py:10
  16.1 0.8 copy.93
  17.0 0.1 eq.44
  17.1 0.1 eq.40
  17.3 0.7 convert_element_type.55
  17.9 0.8 collective-permute-done
  18.7 0.1 multiply_add_fusion.5
  18.8 4.4 collective-permute-start.1
  23.2 1.2 reduce-window.16
  24.4 1.4 collective-permute-done.1
  25.8 0.1 multiply_add_fusion.4
  25.9 4.4 collective-permute-start.2
  30.3 0.2 slice_reduce_fusion
  30.6 0.1 fusion.32
  30.7 2.2 collective-permute-done.2
  32.9 0.1 multiply_add_fusion.3
  33.0 4.4 collective-permute-start.3
  37.4 0.1 sub.33
  37.6 1.1 copy.81
  38.7 1.3 collective-permute-done.3
  40.0 0.1 multiply_add_fusion.2
  40.1 4.4 collective-permute-start.4
  44.5 0.7 multiply_add_fusion.6
  45.2 1.9 collective-permute-done.4
  47.1 0.1 multiply_add_fusion.1
  47.1 4.4 collective-permute-start.5
  51.6 0.5 fusion.18
  52.0 2.1 collective-permute-done.5
  54.1 0.1 multiply_add_fusion
  54.2 4.4 collective-permute-start.6
  58.6 0.5 fusion.14
  59.1 2.1 collective-permute-done.6
  61.2 0.4 multiply_reduce_fusion
  61.7 0.2 copy.92
  61.9 0.4 convolution_convert_fusion
  62.4 18.3 %all_to_all.15 = bf16[8,2,64,384]{3,2,1,0:T(8,128)(2,1)S(1)} all-to-all(bf16[8,2,64,384]{3,2,1,0:T(8,128)(2,1)S(1)} %bitcast.117), channel_id=1, replica_groups=mesh['seq'=8,'exp'=16] {'seq'}, dimensions={0} | all-to-all | bytes 1572864 | tf_op jit(solution)/shard_map/all_to_all | solution.py:84
  80.6 0.1 copy.97
  80.7 6.7 %stack.2 = bf16[16,8,2,64,384]{4,3,1,2,0:T(8,128)(2,1)} broadcast(bf16[8,2,64,384]{3,2,0,1:T(8,128)(2,1)S(1)} %copy.97), dimensions={1,2,3,4} | broadcast | bytes 13369344 | tf_op jit(solution)/shard_map/stack | solution.py:82
  87.4 146.2 %all_to_all.16 = bf16[16,8,2,64,384]{4,3,1,2,0:T(8,128)(2,1)S(1)} all-to-all(bf16[16,8,2,64,384]{4,3,1,2,0:T(8,128)(2,1)} %stack.2), channel_id=1, replica_groups=mesh['seq'=8,'exp'=16] {'exp'}, dimensions={0} | all-to-all | bytes 25165824 | tf_op jit(solution)/shard_map/all_to_all | solution.py:81
  233.7 3.2 copy.114
  236.9 11.6 %fusion.3 = f32[2,8,64,288]{3,2,1,0:T(8,128)S(1)} fusion(bf16[8,2,64,6144]{3,2,0,1:T(8,128)(2,1)S(1)} %bitcast.112, bf16[2,6144,288]{1,2,0:T(8,128)(2,1)} %param.19), kind=kOutput, calls=%fused_computation.4 | convolution fusion | flops 3623878656 | bytes 20840448 | tf_op jit(solution)/shard_map/sjcd,jdf->sjcf/dot_general | solution.py:93
  248.5 8.9 %fusion.6 = bf16[8,2,64,288]{3,2,0,1:T(8,128)(2,1)S(1)} fusion(f32[2,8,64,288]{3,2,1,0:T(8,128)S(1)} %fusion.3, bf16[8,2,64,6144]{3,2,0,1:T(8,128)(2,1)S(1)} %bitcast.113, bf16[2,6144,288]{1,2,0:T(8,128)(2,1)} %param.20), kind=kOutput, calls=%fused_computation.9 | convolution fusion | flops 3625648128 | bytes 21430272 | tf_op jit(solution)/shard_map/sjcd,jdf->sjcf/dot_general | solution.py:96
  257.4 12.6 %convert_bitcast_fusion = bf16[6144,8,2,64]{0,3,1,2:T(8,128)(2,1)} fusion(bf16[8,2,64,288]{3,2,0,1:T(8,128)(2,1)S(1)} %fusion.6, bf16[2,288,6144]{2,1,0:T(8,128)(2,1)} %param.21), kind=kOutput, calls=%fused_computation | convolution fusion | flops 3630170112 | bytes 20250624 | tf_op jit(solution)/shard_map/sjcf,jfd->dsjc/dot_general | solution.py:100
  270.0 29.7 %copy.110 = bf16[6144,8,2,64]{3,1,2,0:T(8,128)(2,1)} copy(bf16[6144,8,2,64]{0,3,1,2:T(8,128)(2,1)} %convert_bitcast_fusion) | data formatting | bytes 25165824
  299.7 33.4 %reshape.138 = bf16[6144,1024]{1,0:T(8,128)(2,1)} reshape(bf16[6144,2,8,64]{3,2,1,0:T(8,128)(2,1)} %bitcast.111) | data formatting | bytes 25165824
  333.1 7.9 %fusion.29 = f32[2,1,8,64]{3,1,2,0:T(1,128)S(1)} fusion(bf16[8,2,64,6144]{3,2,0,1:T(8,128)(2,1)} %bitcast.114, bf16[6144,2,1,1]{0,1,2,3:T(2,128)(2,1)S(1)} %bitcast.110), kind=kOutput, calls=%fused_computation.49 | convolution fusion | flops 12582912 | bytes 12611584 | tf_op jit(solution)/shard_map/sjcd,dj->sjc/dot_general | solution.py:97
  341.0 83.5 %reduce-scatter.4.cloned.1.call-done = bf16[384,1024]{1,0:T(8,128)(2,1)} async-done(((bf16[6144,1024]{1,0:T(8,128)(2,1)}), bf16[384,1024]{1,0:T(8,128)(2,1)}) %reduce-scatter.4.cloned.1.call-update) | async-done | bytes 786448
  424.6 2.5 reshape.139
  427.1 1.2 copy.111
  428.3 0.2 multiply_convert_fusion
  428.5 0.1 copy.99
  428.6 17.3 %all_to_all.17 = bf16[384,8,2,64]{0,3,2,1:T(8,128)(2,1)S(1)} all-to-all(bf16[384,8,2,64]{0,3,2,1:T(8,128)(2,1)S(1)} %copy.99), channel_id=1, replica_groups=mesh['seq'=8,'exp'=16] {'seq'}, dimensions={1} | all-to-all | bytes 1572864 | tf_op jit(solution)/shard_map/all_to_all | solution.py:108
  445.9 1.1 fusion.17
  (23 shorter events, 0.4 us)
Async XLA Ops:
  6.5 326.6 %copy-start = (bf16[6144,2]{0,1:T(2,128)(2,1)S(1)}, bf16[6144,2]{0,1:T(2,128)(2,1)}, u32[]{:S(2)}) copy-start(bf16[6144,2]{0,1:T(2,128)(2,1)} %param.18) | copy-start | bytes 73732
  6.5 55.3 %copy-start.2 = (bf16[256,384]{1,0:T(8,128)(2,1)S(1)}, bf16[256,384]{1,0:T(8,128)(2,1)}, u32[]{:S(2)}) copy-start(bf16[256,384]{1,0:T(8,128)(2,1)} %param.15) | copy-start | bytes 589828
  6.5 418.0 %reduce-scatter.4.cloned.1.call-start = ((), (), s32[]{:S(2)}) async-start(), calls=%async_computation.4 | async-start | bytes 13369344
  11.2 7.5 %collective-permute-start = (f32[3,128,128]{2,1,0:T(8,128)S(1)}, f32[3,128,128]{2,1,0:T(8,128)S(1)}, u32[]{:S(2)}, u32[]{:S(2)}) collective-permute-start(f32[3,128,128]{2,1,0:T(8,128)S(1)} %get-tuple-element.9), channel_id=1, source_target_pairs={{0,16},{16,32},{32,48},{48,64},{64,80},{80,96},{96,112},{1,17},{17... | collective-permute-start | bytes 589832 | tf_op jit(solution)/shard_map/ppermute | solution.py:10
  18.8 7.0 %collective-permute-start.1 = (f32[3,128,128]{2,1,0:T(8,128)S(1)}, f32[3,128,128]{2,1,0:T(8,128)S(1)}, u32[]{:S(2)}, u32[]{:S(2)}) collective-permute-start(f32[3,128,128]{2,1,0:T(8,128)S(1)} %multiply_add_fusion.5), channel_id=1, source_target_pairs={{0,16},{16,32},{32,48},{48,64},{64,80},{80,96},{96,112},{1,17},{17... | collective-permute-start | bytes 589832 | tf_op jit(solution)/shard_map/ppermute | solution.py:10
  25.9 7.0 %collective-permute-start.2 = (f32[3,128,128]{2,1,0:T(8,128)S(1)}, f32[3,128,128]{2,1,0:T(8,128)S(1)}, u32[]{:S(2)}, u32[]{:S(2)}) collective-permute-start(f32[3,128,128]{2,1,0:T(8,128)S(1)} %multiply_add_fusion.4), channel_id=1, source_target_pairs={{0,16},{16,32},{32,48},{48,64},{64,80},{80,96},{96,112},{1,17},{17... | collective-permute-start | bytes 589832 | tf_op jit(solution)/shard_map/ppermute | solution.py:10
  33.0 7.0 %collective-permute-start.3 = (f32[3,128,128]{2,1,0:T(8,128)S(1)}, f32[3,128,128]{2,1,0:T(8,128)S(1)}, u32[]{:S(2)}, u32[]{:S(2)}) collective-permute-start(f32[3,128,128]{2,1,0:T(8,128)S(1)} %multiply_add_fusion.3), channel_id=1, source_target_pairs={{0,16},{16,32},{32,48},{48,64},{64,80},{80,96},{96,112},{1,17},{17... | collective-permute-start | bytes 589832 | tf_op jit(solution)/shard_map/ppermute | solution.py:10
  40.1 7.0 %collective-permute-start.4 = (f32[3,128,128]{2,1,0:T(8,128)S(1)}, f32[3,128,128]{2,1,0:T(8,128)S(1)}, u32[]{:S(2)}, u32[]{:S(2)}) collective-permute-start(f32[3,128,128]{2,1,0:T(8,128)S(1)} %multiply_add_fusion.2), channel_id=1, source_target_pairs={{0,16},{16,32},{32,48},{48,64},{64,80},{80,96},{96,112},{1,17},{17... | collective-permute-start | bytes 589832 | tf_op jit(solution)/shard_map/ppermute | solution.py:10
  47.1 7.0 %collective-permute-start.5 = (f32[3,128,128]{2,1,0:T(8,128)S(1)}, f32[3,128,128]{2,1,0:T(8,128)S(1)}, u32[]{:S(2)}, u32[]{:S(2)}) collective-permute-start(f32[3,128,128]{2,1,0:T(8,128)S(1)} %multiply_add_fusion.1), channel_id=1, source_target_pairs={{0,16},{16,32},{32,48},{48,64},{64,80},{80,96},{96,112},{1,17},{17... | collective-permute-start | bytes 589832 | tf_op jit(solution)/shard_map/ppermute | solution.py:10
  54.2 7.0 %collective-permute-start.6 = (f32[3,128,128]{2,1,0:T(8,128)S(1)}, f32[3,128,128]{2,1,0:T(8,128)S(1)}, u32[]{:S(2)}, u32[]{:S(2)}) collective-permute-start(f32[3,128,128]{2,1,0:T(8,128)S(1)} %multiply_add_fusion), channel_id=1, source_target_pairs={{0,16},{16,32},{32,48},{48,64},{64,80},{80,96},{96,112},{1,17},{17... | collective-permute-start | bytes 589832 | tf_op jit(solution)/shard_map/ppermute | solution.py:10
  236.9 11.6 %copy-start.1 = (bf16[16,2,8,8,8,384]{5,4,0,3,2,1:T(8,128)(2,1)}, bf16[16,2,8,8,8,384]{5,4,0,3,2,1:T(8,128)(2,1)S(1)}, u32[]{:S(2)}) copy-start(bf16[16,2,8,8,8,384]{5,4,0,3,2,1:T(8,128)(2,1)S(1)} %copy.114) | copy-start | bytes 37748740
Sparse Core Ops, SparseCore 0:
  333.2 91.2 reduce-scatter.3
